TPU v7x, 32 devices: a whole 2x2x4 slice. The times are simulated.
32 devices in a mesh: ctx: 8 (over z, x), ch: 4 (over y, core).
Axes of the slice: x: 2, y: 2, z: 4, core: 2. Of those that a mesh axis runs over, the one named last changes fastest.
Arguments:
- short_conv_input: bfloat16 [1024, 1024], P('ctx', 'ch'), may hold values from -6 to 6
- out_gate: bfloat16 [1024, 1024], P('ctx', 'ch'), may hold values from -6 to 6
- in_gate: bfloat16 [1024, 1024], P('ctx', 'ch'), may hold values from -6 to 6
- out_cotangent: bfloat16 [1024, 1024], P('ctx', 'ch'), may hold values from -6 to 6
- mr_filter: bfloat16 [128, 64], P(None, 'ch'), may hold values from -0.5 to 0.5
- residues: float32 [16, 1024], P(None, ('ch', 'ctx')), may hold values from -5 to 5
- rates: float32 [16, 1024], P(None, ('ch', 'ctx')), may hold values from 0.0009765625 to 0.03
Outputs:
- input_grad: bfloat16 [1024, 1024], P('ctx', 'ch')
- out_gate_grad: bfloat16 [1024, 1024], P('ctx', 'ch')
- in_gate_grad: bfloat16 [1024, 1024], P('ctx', 'ch')
- filter_grad: float32 [128, 64], P(None, 'ch')
- residue_grad: float32 [16, 1024], P(None, ('ch', 'ctx'))
- rate_grad: float32 [16, 1024], P(None, ('ch', 'ctx'))
All inputs are finite; a program needn't handle non-finite values.
Results may differ from a plain program's by a relative error of at most 0.013.
Values may be sent and summed in bfloat16 or wider, within the bound.
A program may use at most 64 MiB of HBM per device.

v0:
```python
import math

import jax
import jax.numpy as jnp
from jax import lax
from jax.sharding import PartitionSpec as P

HIGHEST = lax.Precision.HIGHEST


def from_behind(value, axis, by):
    peers = lax.axis_size(axis)
    pairs = [(i, i + by) for i in range(peers) if 0 <= i + by < peers]
    return lax.ppermute(value, axis, pairs)


def product(left, right):
    return (left.astype(jnp.float32) * right.astype(jnp.float32)).astype(jnp.bfloat16)


def dft_table(count):
    index = jnp.arange(count, dtype=jnp.int32)
    angle = (index[:, None] * index[None, :] % count).astype(jnp.float32) * (-2.0 * math.pi / count)
    return (jnp.cos(angle), jnp.sin(angle))


def twiddle_table(first, second):
    rows = jnp.arange(first, dtype=jnp.int32)
    cols = jnp.arange(second, dtype=jnp.int32)
    total = first * second
    angle = (rows[:, None] * cols[None, :] % total).astype(jnp.float32) * (-2.0 * math.pi / total)
    return (jnp.cos(angle), jnp.sin(angle))


def forward_dft(signal, tables):
    (fa_re, fa_im), (fb_re, fb_im), (tw_re, tw_im) = tables
    y_re = jnp.einsum("ki,cij->ckj", fa_re, signal, precision=HIGHEST)
    y_im = jnp.einsum("ki,cij->ckj", fa_im, signal, precision=HIGHEST)
    p_re = y_re * tw_re - y_im * tw_im
    p_im = y_re * tw_im + y_im * tw_re
    z_re = jnp.einsum("ckj,jl->ckl", p_re, fb_re, precision=HIGHEST) - jnp.einsum(
        "ckj,jl->ckl", p_im, fb_im, precision=HIGHEST
    )
    z_im = jnp.einsum("ckj,jl->ckl", p_re, fb_im, precision=HIGHEST) + jnp.einsum(
        "ckj,jl->ckl", p_im, fb_re, precision=HIGHEST
    )
    return (z_re, z_im)


def inverse_dft(spec_re, spec_im, tables, length):
    (fa_re, fa_im), (fb_re, fb_im), (tw_re, tw_im) = tables
    q_re = jnp.einsum("ckl,jl->ckj", spec_re, fb_re, precision=HIGHEST) + jnp.einsum(
        "ckl,jl->ckj", spec_im, fb_im, precision=HIGHEST
    )
    q_im = jnp.einsum("ckl,jl->ckj", spec_im, fb_re, precision=HIGHEST) - jnp.einsum(
        "ckl,jl->ckj", spec_re, fb_im, precision=HIGHEST
    )
    s_re = q_re * tw_re + q_im * tw_im
    s_im = q_im * tw_re - q_re * tw_im
    signal = jnp.einsum("ik,ckj->cij", fa_re, s_re, precision=HIGHEST) + jnp.einsum(
        "ik,ckj->cij", fa_im, s_im, precision=HIGHEST
    )
    total = signal.shape[1] * signal.shape[2]
    return signal.reshape(signal.shape[0], total)[:, :length] / total


def long_mixer(u_cols, dz_cols, residues, rates):
    length, width = u_cols.shape
    total = 2 * length
    first = math.gcd(total, 2 ** (total.bit_length() // 2))
    second = total // first
    tables = (dft_table(first), dft_table(second), twiddle_table(first, second))

    def spread(rows):
        padded = jnp.concatenate([rows, jnp.zeros_like(rows)], axis=1)
        return padded.reshape(width, first, second)

    norm = jnp.sqrt(2.0 * rates / rates.shape[0])
    weights = residues * norm
    tau = jnp.arange(length).astype(jnp.float32)

    def add_mode(acc, pair):
        weight, rate = pair
        return (acc + weight[:, None] * jnp.exp(-rate[:, None] * tau[None, :]), None)

    filt, _ = lax.scan(add_mode, jnp.zeros((width, length), jnp.float32), (weights, rates))
    h_re, h_im = forward_dft(spread(filt), tables)
    u_re, u_im = forward_dft(spread(u_cols.astype(jnp.float32).T), tables)
    d_re, d_im = forward_dft(spread(dz_cols.astype(jnp.float32).T), tables)
    conv = inverse_dft(h_re * u_re - h_im * u_im, h_re * u_im + h_im * u_re, tables, length)
    back = inverse_dft(h_re * d_re + h_im * d_im, h_re * d_im - h_im * d_re, tables, length)
    filt_grad = inverse_dft(u_re * d_re + u_im * d_im, u_re * d_im - u_im * d_re, tables, length)

    def mode_sums(rate):
        decay = jnp.exp(-rate[:, None] * tau[None, :])
        first_sum = jnp.sum(filt_grad * decay, axis=1)
        second_sum = jnp.sum(filt_grad * decay * tau[None, :], axis=1)
        return (first_sum, second_sum)

    s_first, s_second = lax.map(mode_sums, rates)
    scale = 1.0 / math.sqrt(length)
    residue_grad = norm * s_first * scale
    rate_grad = weights * (0.5 * s_first - rates * s_second) * scale
    return (conv.T.astype(jnp.bfloat16), back.T.astype(jnp.bfloat16), residue_grad, rate_grad)


def make_windows(extended, taps):
    count = extended.shape[0] // taps
    blocks = extended.reshape(count, taps, extended.shape[1])
    return jnp.concatenate([blocks[:-1], blocks[1:]], axis=1)


def toeplitz(filt, taps, causal):
    rows = jnp.arange(taps, dtype=jnp.int32)[:, None]
    cols = jnp.arange(2 * taps, dtype=jnp.int32)[None, :]
    if causal:
        lag = taps + rows - cols
    else:
        lag = cols - rows
    tap_index = jnp.arange(taps, dtype=jnp.int32)
    selector = (lag[:, :, None] == tap_index[None, None, :]).astype(filt.dtype)
    table = jnp.einsum("bkj,jg->gbk", selector, filt, preferred_element_type=jnp.float32)
    return table.astype(filt.dtype)


def local(short_conv_input, out_gate, in_gate, out_cotangent, mr_filter, residues, rates):
    taps = mr_filter.shape[0]
    tok_rows, chans = short_conv_input.shape
    local_groups = mr_filter.shape[1]
    group_width = chans // local_groups
    blocks = tok_rows // taps
    x_rim = from_behind(short_conv_input, "ctx", 1)
    x_windows = make_windows(jnp.concatenate([x_rim, short_conv_input], axis=0), taps).reshape(
        blocks, 2 * taps, local_groups, group_width
    )
    causal = toeplitz(mr_filter, taps, True)
    mr_output = (
        jnp.einsum("gbk,nkgs->nbgs", causal, x_windows, preferred_element_type=jnp.float32)
        .reshape(tok_rows, chans)
        .astype(jnp.bfloat16)
    )
    gated = product(in_gate, mr_output)
    gated_cot = product(out_gate, out_cotangent)
    u_cols, dz_cols = (
        lax.all_to_all(gated, "ctx", split_axis=1, concat_axis=0, tiled=True),
        lax.all_to_all(gated_cot, "ctx", split_axis=1, concat_axis=0, tiled=True),
    )
    z_cols, du_cols, residue_grad, rate_grad = long_mixer(u_cols, dz_cols, residues, rates)
    conv, back = (
        lax.all_to_all(z_cols, "ctx", split_axis=0, concat_axis=1, tiled=True),
        lax.all_to_all(du_cols, "ctx", split_axis=0, concat_axis=1, tiled=True),
    )
    out_gate_grad = product(out_cotangent, conv)
    in_gate_grad = product(back, mr_output)
    mr_out_grad = product(back, in_gate)
    dv_rim = from_behind(mr_out_grad, "ctx", -1)
    dv_windows = make_windows(jnp.concatenate([mr_out_grad, dv_rim], axis=0), taps).reshape(
        blocks, 2 * taps, local_groups, group_width
    )
    anti = toeplitz(mr_filter, taps, False)
    input_grad = (
        jnp.einsum("gbk,nkgs->nbgs", anti, dv_windows, preferred_element_type=jnp.float32)
        .reshape(tok_rows, chans)
        .astype(jnp.bfloat16)
    )
    corr = jnp.einsum(
        "nbgs,nkgs->gbk",
        mr_out_grad.reshape(blocks, taps, local_groups, group_width),
        x_windows,
        preferred_element_type=jnp.float32,
    )
    flat = jnp.pad(corr.reshape(local_groups, taps * 2 * taps), ((0, 0), (0, taps)))
    diagonals = jnp.sum(flat.reshape(local_groups, taps, 2 * taps + 1), axis=1)
    local_sums = diagonals[:, taps:0:-1].T
    tokens_all = tok_rows * lax.axis_size("ctx")
    filter_grad = lax.psum(local_sums, "ctx") * (1.0 / math.sqrt(tokens_all))
    return (input_grad, out_gate_grad, in_gate_grad, filter_grad, residue_grad, rate_grad)


def solution(mesh):
    return jax.shard_map(
        local,
        mesh=mesh,
        in_specs=(
            P("ctx", "ch"),
            P("ctx", "ch"),
            P("ctx", "ch"),
            P("ctx", "ch"),
            P(None, "ch"),
            P(None, ("ch", "ctx")),
            P(None, ("ch", "ctx")),
        ),
        out_specs=(
            P("ctx", "ch"),
            P("ctx", "ch"),
            P("ctx", "ch"),
            P(None, "ch"),
            P(None, ("ch", "ctx")),
            P(None, ("ch", "ctx")),
        ),
        check_vma=False,
    )
```

profile of v0, /device:TPU:0, one launch (start us, length us, event | category | flops | bytes accessed | tf_op | source)
XLA Modules:
  0.0 145.7 jit_solution(9162200252311635012)
XLA Ops:
  3.2 7.3 %all-to-all-start = ((bf16[128,8,32]{0,2,1:T(8,128)(2,1)}), bf16[128,8,32]{0,2,1:T(8,128)(2,1)S(1)}, u32[]{:S(2)}, u32[]{:S(2)}) async-start(bf16[128,8,32]{0,2,1:T(8,128)(2,1)} %bitcast.6), calls=%async_computation | async-start | bytes 131072 | tf_op jit(solution)/shard_map/all_to_all | solution.py:146
  10.5 3.9 %collective-permute-start.1 = (bf16[128,256]{1,0:T(8,128)(2,1)}, bf16[128,256]{1,0:T(8,128)(2,1)S(1)}, u32[]{:S(2)}, u32[]{:S(2)}) collective-permute-start(bf16[128,256]{1,0:T(8,128)(2,1)} %param.11), channel_id=1, source_target_pairs={{0,4},{4,8},{8,12},{12,16},{16,20},{20,24},{24,28},{1,5},{5,9},{9,... | collective-permute-start | bytes 196616 | tf_op jit(solution)/shard_map/ppermute | solution.py:14
  15.3 13.3 %while.26 = (s32[]{:T(128)}, f32[32,1024]{1,0:T(8,128)S(1)}, f32[16,32]{1,0:T(8,128)S(1)}, f32[16,32]{1,0:T(8,128)}, s32[]{:T(128)}, /*index=5*/s32[]{:T(128)}) while((s32[]{:T(128)}, f32[32,1024]{1,0:T(8,128)S(1)}, f32[16,32]{1,0:T(8,128)S(1)}, f32[16,32]{1,0:T(8,128)}, s32[]{:T(128)}, /*index=5*/s32[]{:T(128)}) %tuple.63), condition=%wide.region_1.2_spmd.clone, body=%wide.region_0.1_spmd.clone.sunk | while | flops 132131 | bytes 271195 | solution.py:86
  29.0 1.8 %convolution_bitcast_fusion.4 = f32[32,64,32]{1,2,0:T(8,128)S(1)} fusion(f32[32,64,32]{2,1,0:T(8,128)S(1)} %reshape.197), kind=kOutput, calls=%fused_computation.41 | convolution fusion | flops 50388992 | bytes 524288 | tf_op jit(solution)/shard_map/ki,cij->ckj/dot_general | solution.py:38
  30.8 1.8 %convolution_bitcast_fusion.5 = f32[32,64,32]{1,2,0:T(8,128)S(1)} fusion(f32[32,64,32]{2,1,0:T(8,128)S(1)} %reshape.197), kind=kOutput, calls=%fused_computation.42 | convolution fusion | flops 50388992 | bytes 524288 | tf_op jit(solution)/shard_map/ki,cij->ckj/dot_general | solution.py:37
  35.6 8.2 %fusion.5 = bf16[128,256,16]{1,2,0:T(8,128)(2,1)} fusion(s32[128,256]{1,0:T(8,128)S(1)} %iota_subtract_fusion.1, bf16[128,16]{0,1:T(8,128)(2,1)S(1)} %copy-done), kind=kOutput, calls=%fused_computation.13 | convolution fusion | flops 138412032 | bytes 1183744 | tf_op jit(solution)/shard_map/bkj,jg->gbk/dot_general | solution.py:122
  43.8 7.4 %fusion.6 = bf16[128,256,16]{1,2,0:T(8,128)(2,1)S(1)} fusion(s32[128,256]{1,0:T(8,128)S(1)} %iota_subtract_fusion, bf16[128,16]{0,1:T(8,128)(2,1)S(1)} %copy-done), kind=kOutput, calls=%fused_computation.14 | convolution fusion | flops 138412032 | bytes 1183744 | tf_op jit(solution)/shard_map/bkj,jg->gbk/dot_general | solution.py:122
  52.7 4.6 %all-to-all-start.2 = ((bf16[128,8,32]{0,2,1:T(8,128)(2,1)}), bf16[128,8,32]{0,2,1:T(8,128)(2,1)S(1)}, u32[]{:S(2)}, u32[]{:S(2)}) async-start(bf16[128,8,32]{0,2,1:T(8,128)(2,1)} %bitcast.38), calls=%async_computation.2 | async-start | bytes 131072 | tf_op jit(solution)/shard_map/all_to_all | solution.py:145
  60.4 1.6 %convolution_add_fusion.7 = f32[32,64,32]{1,2,0:T(8,128)} fusion(f32[32,64,32]{1,2,0:T(8,128)S(1)} %fusion.53, f32[32,64,32]{1,2,0:T(8,128)S(1)} %convolution_bitcast_fusion.2, f32[32,64,32]{1,2,0:T(8,128)S(1)} %convolution_bitcast_fusion.3, f32[64,32]{0,1:T(8,128)S(1)} %get-tuple-element.165, f32[64,32]{0,1:T(8,128)S(1)} %get-tuple-element.166), kind=kOutput, calls=%fused_computation.37 | convolution fusion | flops 25442304 | bytes 1064960 | tf_op jit(solution)/shard_map/ckj,jl->ckl/dot_general | solution.py:44
  62.0 1.6 %convolution_subtract_fusion.4 = f32[32,64,32]{1,2,0:T(8,128)} fusion(f32[32,64,32]{1,2,0:T(8,128)S(1)} %fusion.54, f32[32,64,32]{1,2,0:T(8,128)S(1)} %convolution_bitcast_fusion.2, f32[32,64,32]{1,2,0:T(8,128)S(1)} %convolution_bitcast_fusion.3, f32[64,32]{0,1:T(8,128)S(1)} %get-tuple-element.165, f32[64,32]{0,1:T(8,128)S(1)} %get-tuple-element.166), kind=kOutput, calls=%fused_computation.39 | convolution fusion | flops 25442304 | bytes 1064960 | tf_op jit(solution)/shard_map/ckj,jl->ckl/dot_general | solution.py:41
  68.0 1.1 multiply_add_fusion
  72.8 1.5 %fusion.9 = f32[32,64,32]{1,2,0:T(8,128)} fusion(f32[32,32,64]{2,1,0:T(8,128)S(1)} %fusion.21, f32[32,64,32]{1,2,0:T(8,128)S(1)} %convolution_add_fusion.1, f32[32,64,32]{1,2,0:T(8,128)S(1)} %convolution_subtract_fusion, f32[64,32]{0,1:T(8,128)S(1)} %get-tuple-element.165, f32[64,32]{0,1:T(8,128)S(1)} %get-tuple-element.166), kind=kOutput, calls=%fused_computation.24 | convolution fusion | flops 50651136 | bytes 1064960 | tf_op jit(solution)/shard_map/ik,ckj->cij/dot_general | solution.py:60
  74.3 1.4 copy.64
  75.7 1.2 reshape.209
  77.8 5.2 %while.25 = (s32[]{:T(128)}, f32[16,32]{1,0:T(8,128)S(1)}, f32[16,32]{1,0:T(8,128)S(1)}, f32[16,32]{1,0:T(8,128)S(1)}, f32[32,1024]{1,0:T(8,128)S(1)}, /*index=5*/s32[]{:T(128)}, s32[]{:T(128)}) while((s32[]{:T(128)}, f32[16,32]{1,0:T(8,128)S(1)}, f32[16,32]{1,0:T(8,128)S(1)}, f32[16,32]{1,0:T(8,128)S(1)}, ...), condition=%wide.region_7.8_spmd.clone.clone, body=%wide.region_4.7_spmd.clone.clone.sunk | while | flops 164834 | bytes 140513 | solution.py:100
  88.7 5.4 %all-to-all-start.1 = ((bf16[8,128,32]{1,2,0:T(8,128)(2,1)}), bf16[8,128,32]{1,2,0:T(8,128)(2,1)S(1)}, u32[]{:S(2)}, u32[]{:S(2)}) async-start(bf16[8,128,32]{1,2,0:T(8,128)(2,1)} %copy_bitcast_fusion.1), calls=%async_computation.1 | async-start | bytes 131072 | tf_op jit(solution)/shard_map/all_to_all | solution.py:151
  101.0 5.3 %all-to-all-start.3 = ((bf16[8,128,32]{1,2,0:T(8,128)(2,1)}), bf16[8,128,32]{1,2,0:T(8,128)(2,1)}, u32[]{:S(2)}, u32[]{:S(2)}) async-start(bf16[8,128,32]{1,2,0:T(8,128)(2,1)} %copy_bitcast_fusion), calls=%async_computation.3 | async-start | bytes 131072 | tf_op jit(solution)/shard_map/all_to_all | solution.py:150
  107.0 1.5 %collective-permute-start = (bf16[128,256]{0,1:T(8,128)(2,1)}, bf16[128,256]{0,1:T(8,128)(2,1)}, u32[]{:S(2)}, u32[]{:S(2)}) collective-permute-start(bf16[128,256]{0,1:T(8,128)(2,1)} %get-tuple-element.162), channel_id=1, source_target_pairs={{4,0},{8,4},{12,8},{16,12},{20,16},{24,20},{28,24},{5,1},{9,5},{13... | collective-permute-start | bytes 196616 | tf_op jit(solution)/shard_map/ppermute | solution.py:14
  108.5 1.3 fusion.66
  109.9 1.2 copy.104
  111.1 1.4 pad.9
  112.5 3.7 %reshape.208 = f32[16,128,257]{2,1,0:T(8,128)S(1)} reshape(f32[16,32896]{1,0:T(8,128)} %pad.9) | data formatting | bytes 4210688 | tf_op jit(solution)/shard_map/reshape | solution.py:173
  116.7 23.6 %psum.7 = f32[128,16]{0,1:T(8,128)S(1)} all-reduce(f32[128,16]{0,1:T(8,128)S(1)} %bitcast.234), channel_id=1, replica_groups=mesh['ctx'=8,'ch'=4] {'ctx'}, use_global_device_ids=true, to_apply=%region_3.4 | all-reduce | flops 2048 | bytes 16384 | tf_op jit(solution)/shard_map/psum | solution.py:176
  143.2 1.7 %convolution_convert_fusion.1 = bf16[16,16,128]{2,1,0:T(8,128)(2,1)S(1)} fusion(bf16[128,256,16]{1,2,0:T(8,128)(2,1)} %fusion.5, bf16[1,128,16,16]{1,3,2,0:T(8,128)(2,1)} %bitcast.24, bf16[1,128,16,16]{1,3,2,0:T(8,128)(2,1)} %bitcast.23), kind=kOutput, calls=%fused_computation.44 | convolution fusion | flops 17072128 | bytes 1245184 | tf_op jit(solution)/shard_map/gbk,nkgs->nbgs/dot_general | solution.py:162
  (225 shorter events, 55.1 us)
Async XLA Ops:
  0.6 35.0 %copy-start = (bf16[128,16]{0,1:T(8,128)(2,1)S(1)}, bf16[128,16]{0,1:T(8,128)(2,1)}, u32[]{:S(2)}) copy-start(bf16[128,16]{0,1:T(8,128)(2,1)} %param.15) | copy-start | bytes 12292
  3.2 49.5 %all-to-all-start = ((bf16[128,8,32]{0,2,1:T(8,128)(2,1)}), bf16[128,8,32]{0,2,1:T(8,128)(2,1)S(1)}, u32[]{:S(2)}, u32[]{:S(2)}) async-start(bf16[128,8,32]{0,2,1:T(8,128)(2,1)} %bitcast.6), calls=%async_computation | async-start | bytes 131072 | tf_op jit(solution)/shard_map/all_to_all | solution.py:146
  10.5 41.0 %collective-permute-start.1 = (bf16[128,256]{1,0:T(8,128)(2,1)}, bf16[128,256]{1,0:T(8,128)(2,1)S(1)}, u32[]{:S(2)}, u32[]{:S(2)}) collective-permute-start(bf16[128,256]{1,0:T(8,128)(2,1)} %param.11), channel_id=1, source_target_pairs={{0,4},{4,8},{8,12},{12,16},{16,20},{20,24},{24,28},{1,5},{5,9},{9,... | collective-permute-start | bytes 196616 | tf_op jit(solution)/shard_map/ppermute | solution.py:14
  43.8 7.4 %copy-start.7 = (bf16[128,256]{1,0:T(8,128)(2,1)S(1)}, bf16[128,256]{1,0:T(8,128)(2,1)}, u32[]{:S(2)}) copy-start(bf16[128,256]{1,0:T(8,128)(2,1)} %param.11) | copy-start | bytes 196612
  43.8 7.6 %copy-start.6 = (bf16[128,256]{1,0:T(8,128)(2,1)S(1)}, bf16[128,256]{1,0:T(8,128)(2,1)}, u32[]{:S(2)}) copy-start(bf16[128,256]{1,0:T(8,128)(2,1)} %param.13) | copy-start | bytes 196612
  51.5 8.2 %copy-start.3 = (bf16[128,256]{0,1:T(8,128)(2,1)}, bf16[128,256]{0,1:T(8,128)(2,1)S(1)}, u32[]{:S(2)}) copy-start(bf16[128,256]{0,1:T(8,128)(2,1)S(1)} %copy.52) | copy-start | bytes 196612
  52.7 11.5 %all-to-all-start.2 = ((bf16[128,8,32]{0,2,1:T(8,128)(2,1)}), bf16[128,8,32]{0,2,1:T(8,128)(2,1)S(1)}, u32[]{:S(2)}, u32[]{:S(2)}) async-start(bf16[128,8,32]{0,2,1:T(8,128)(2,1)} %bitcast.38), calls=%async_computation.2 | async-start | bytes 131072 | tf_op jit(solution)/shard_map/all_to_all | solution.py:145
  65.2 2.8 %copy-start.1 = (f32[32,64,32]{1,2,0:T(8,128)S(1)}, f32[32,64,32]{1,2,0:T(8,128)}, u32[]{:S(2)}) copy-start(f32[32,64,32]{1,2,0:T(8,128)} %convolution_add_fusion.7) | copy-start | bytes 786436
  65.2 2.8 %copy-start.2 = (f32[32,64,32]{1,2,0:T(8,128)S(1)}, f32[32,64,32]{1,2,0:T(8,128)}, u32[]{:S(2)}) copy-start(f32[32,64,32]{1,2,0:T(8,128)} %convolution_subtract_fusion.4) | copy-start | bytes 786436
  71.8 6.1 %copy-start.8 = (f32[16,32]{1,0:T(8,128)S(1)}, f32[16,32]{1,0:T(8,128)}, u32[]{:S(2)}) copy-start(f32[16,32]{1,0:T(8,128)} %get-tuple-element.275) | copy-start | bytes 6148
  88.7 12.3 %all-to-all-start.1 = ((bf16[8,128,32]{1,2,0:T(8,128)(2,1)}), bf16[8,128,32]{1,2,0:T(8,128)(2,1)S(1)}, u32[]{:S(2)}, u32[]{:S(2)}) async-start(bf16[8,128,32]{1,2,0:T(8,128)(2,1)} %copy_bitcast_fusion.1), calls=%async_computation.1 | async-start | bytes 131072 | tf_op jit(solution)/shard_map/all_to_all | solution.py:151
  96.7 3.0 %copy-start.9 = (f32[16,32]{1,0:T(8,128)S(1)}, f32[16,32]{1,0:T(8,128)}, u32[]{:S(2)}) copy-start(f32[16,32]{1,0:T(8,128)} %param.16) | copy-start | bytes 6148
  96.7 9.6 %copy-start.4 = (bf16[128,256]{0,1:T(8,128)(2,1)S(1)}, bf16[128,256]{0,1:T(8,128)(2,1)}, u32[]{:S(2)}) copy-start(bf16[128,256]{0,1:T(8,128)(2,1)} %copy-done.3) | copy-start | bytes 196612
  101.0 39.3 %all-to-all-start.3 = ((bf16[8,128,32]{1,2,0:T(8,128)(2,1)}), bf16[8,128,32]{1,2,0:T(8,128)(2,1)}, u32[]{:S(2)}, u32[]{:S(2)}) async-start(bf16[8,128,32]{1,2,0:T(8,128)(2,1)} %copy_bitcast_fusion), calls=%async_computation.3 | async-start | bytes 131072 | tf_op jit(solution)/shard_map/all_to_all | solution.py:150
  107.0 36.2 %collective-permute-start = (bf16[128,256]{0,1:T(8,128)(2,1)}, bf16[128,256]{0,1:T(8,128)(2,1)}, u32[]{:S(2)}, u32[]{:S(2)}) collective-permute-start(bf16[128,256]{0,1:T(8,128)(2,1)} %get-tuple-element.162), channel_id=1, source_target_pairs={{4,0},{8,4},{12,8},{16,12},{20,16},{24,20},{28,24},{5,1},{9,5},{13... | collective-permute-start | bytes 196616 | tf_op jit(solution)/shard_map/ppermute | solution.py:14
  112.5 29.2 %copy-start.5 = (bf16[128,256]{0,1:T(8,128)(2,1)S(1)}, bf16[128,256]{0,1:T(8,128)(2,1)}, u32[]{:S(2)}) copy-start(bf16[128,256]{0,1:T(8,128)(2,1)} %get-tuple-element.161) | copy-start | bytes 196612
where the time goes:
time: 147 us; the launch traced here: 146 us
  matrix products  49 us (33%)
  starting transfers between devices  28 us (19%)
  other arithmetic  24 us (16%)
  blocking collectives  23.6 us (16%)
  local copies, waits for them, and re-layouts  17.7 us (12%)
    psum x1, blocking collectives, local(): filter_grad = lax.psum(local_sums, 'ctx') * (1.0 / math.sqrt(tokens_all))  23.6 us
    dot_general x2, matrix products, toeplitz(): jnp.einsum('bkj,jg->gbk', selector, filt, preferred_element_type=jnp.floa...  15.6 us
    neg x16, other arithmetic, add_mode(): -rate[:, None] * tau[None, :]  11.2 us
    all_to_all x1, starting transfers between devices, local(): lax.all_to_all(gated_cot, 'ctx', split_axis=1, concat_axis=0, tiled=True)  7.28 us
    unnamed x28, local copies, waits for them, and re-layouts  5.64 us
    ppermute x2, starting transfers between devices, from_behind(): return lax.ppermute(value, axis, pairs)  5.46 us
    all_to_all x1, starting transfers between devices, local(): lax.all_to_all(du_cols, 'ctx', split_axis=0, concat_axis=1, tiled=True)  5.39 us
    all_to_all x1, starting transfers between devices, local(): lax.all_to_all(z_cols, 'ctx', split_axis=0, concat_axis=1, tiled=True)  5.34 us
  transfers between devices with their start and end apart: 6, of which 2 were waited for; matrix products, arithmetic and copies ran while one was open for 42% of the time, Pallas kernels for 0%

commit v1 on v0

v1 whole, which is shorter than its diff:
```python
import functools
import math

import jax
import jax.numpy as jnp
import numpy as np
from jax import lax
from jax.experimental import pallas as pl
from jax.experimental.pallas import tpu as pltpu
from jax.sharding import PartitionSpec as P

MESH = pl.DeviceIdType.MESH
F32, BF16 = jnp.float32, jnp.bfloat16
AXIS = "ctx"


def dft_tables(half):
    size = 2 * half
    k = np.arange(half)[:, None]
    t = np.arange(half)[None, :]
    angle = 2.0 * np.pi * (k * t % size) / size
    real, imag = np.cos(angle), -np.sin(angle)
    imag[0] = np.cos(np.pi * np.arange(half))
    forward = np.concatenate([real, imag], axis=0)
    gain = np.full((size, 1), 2.0 / size)
    gain[0] = gain[half] = 1.0 / size
    inverse = (forward * gain).T

    def split(table):
        table = table.astype(np.float32)
        high = table.astype(BF16)
        return high, (table - high.astype(np.float32)).astype(BF16)

    return np.concatenate(split(forward), axis=1), np.concatenate(split(inverse), axis=0)


def dot(left, right):
    return jnp.dot(left, right, preferred_element_type=F32)


def split(value):
    high = value.astype(BF16)
    return high, (value - high.astype(F32)).astype(BF16)


def product(left, right):
    return (left.astype(F32) * right.astype(F32)).astype(BF16)


def kernel(
    n, x_ref, og_ref, ig_ref, oc_ref, filt_ref, res_ref, rate_ref, fwd_ref, inv_ref,
    xg_ref, ogg_ref, igg_ref, fg_ref, rg_ref, tg_ref,
    rim, rr_all, d_all, u_all, dv, dv_rim, mp_send, mp_all, fg_all,
    rates, resid, decay, decay_rev, h_ref, d_sum, u_sum, m_sum, dz_ref, u_ref, g_ref,
    back_ref, conv_ref, xs_ref, fs_ref,
    rim_sem, rr_send, rr_recv, d_send, d_recv, u_send, u_recv, dv_sem, mp_ssem, mp_rsem, fg_send, fg_recv,
):
    me = lax.axis_index(AXIS)
    rows, chans = x_ref.shape
    modes, own = rate_ref.shape
    groups = filt_ref.shape[1]
    parts = modes // 8

    barrier = pltpu.get_barrier_semaphore()

    def greet(k, carry):
        pl.semaphore_signal(barrier, inc=1, device_id={AXIS: lax.rem(me + k, n)}, device_id_type=MESH)
        return carry

    lax.fori_loop(1, n, greet, 0)
    for g in range(parts):
        rr_all[me, :, g * own : (g + 1) * own] = rate_ref[8 * g : 8 * g + 8, :]
        rr_all[me, :, (parts + g) * own : (parts + g + 1) * own] = res_ref[8 * g : 8 * g + 8, :]
    pl.semaphore_wait(barrier, n - 1)

    def remote(src, dst, ssem, rsem, to):
        return pltpu.make_async_remote_copy(
            src_ref=src, dst_ref=dst, send_sem=ssem, recv_sem=rsem, device_id={AXIS: to}, device_id_type=MESH
        )

    def rr_copy(slot, to):
        return remote(rr_all.at[slot], rr_all.at[slot], rr_send.at[to], rr_recv.at[slot], to)

    def fg_copy(slot, to):
        return remote(fg_all.at[slot], fg_all.at[slot], fg_send.at[to], fg_recv.at[slot], to)

    def mp_copy(slot, to):
        return remote(mp_send.at[to], mp_all.at[slot], mp_ssem.at[to], mp_rsem.at[slot], to)

    def d_copy(slot, to):
        return remote(d_all.at[slot], d_all.at[slot], d_send.at[to], d_recv.at[slot], to)

    def u_copy(slot, to):
        return remote(u_all.at[slot], u_all.at[slot], u_send.at[to], u_recv.at[slot], to)

    def rim_copy(to):
        return remote(x_ref, rim, rim_sem.at[0], rim_sem.at[1], to)

    def dv_copy(to):
        return remote(dv, dv_rim, dv_sem.at[0], dv_sem.at[1], to)

    def others(act):
        def step(k, carry):
            act(lax.rem(me + k, n))
            return carry

        lax.fori_loop(1, n, step, 0)

    def span(lo, hi, act):
        def step(j, carry):
            act(j)
            return carry

        lax.fori_loop(lo, hi, step, 0)

    others(lambda j: rr_copy(me, j).start())

    @pl.when(me < n - 1)
    def _():
        rim_copy(me + 1).start()

    fwd = fwd_ref[...]
    fwd_hi = fwd[:, :rows]
    inv_hi = inv_ref[:rows, :]
    inv_lo = inv_ref[rows:, :]
    tau = lax.broadcasted_iota(jnp.int32, (rows, chans), 0)
    first_row = tau == 0
    tau_f = tau.astype(F32)
    left_f = (rows - 1) - tau_f
    sign = (1 - 2 * lax.rem(lax.broadcasted_iota(jnp.int32, (2 * rows, chans), 0), 2)).astype(F32)

    def spectrum(value):
        return dot(fwd, jnp.concatenate([value, value], axis=0))

    def signal(spec):
        high, low = split(spec)
        return dot(inv_hi, high) + dot(inv_hi, low) + dot(inv_lo, high)

    def times(a, b, conj):
        ar, ai, br, bi = a[:rows], a[rows:], b[:rows], b[rows:]
        pure = ai * bi
        cross = jnp.where(first_row, 0.0, pure)
        if conj:
            return jnp.concatenate([ar * br + cross, jnp.where(first_row, pure, ar * bi - ai * br)], axis=0)
        return jnp.concatenate([ar * br - cross, jnp.where(first_row, pure, ar * bi + ai * br)], axis=0)

    member = (
        lax.broadcasted_iota(jnp.int32, (groups, chans), 1) // (chans // groups)
        == lax.broadcasted_iota(jnp.int32, (groups, chans), 0)
    ).astype(BF16)
    taps = dot(filt_ref[...], member).astype(BF16)
    fs_ref[...] = spectrum(taps)
    dz = product(og_ref[...], oc_ref[...])
    dz_ref[...] = dz.astype(F32)
    xs_ref[...] = spectrum(x_ref[...])

    others(lambda j: rr_copy(j, j).wait_recv())
    for j in range(n):
        piece = rr_all[j]
        for g in range(parts):
            rates[8 * g : 8 * g + 8, j * own : (j + 1) * own] = piece[:, g * own : (g + 1) * own]
            resid[8 * g : 8 * g + 8, j * own : (j + 1) * own] = piece[:, (parts + g) * own : (parts + g + 1) * own]

    norm = jnp.sqrt(2.0 * rates[...] / modes)
    resid[...] = resid[...] * norm
    h_ref[...] = jnp.zeros_like(h_ref)

    def build(m, carry):
        rate = rates[pl.ds(m, 1), :]
        e = jnp.exp(-rate * tau_f)
        decay[m] = e
        decay_rev[m] = jnp.exp(-rate * left_f)
        h_ref[...] += resid[pl.ds(m, 1), :] * e
        ed = e * dz_ref[...]
        d_sum[pl.ds(m, 1), :] = jnp.sum(ed, axis=0, keepdims=True)
        d_sum[pl.ds(modes + m, 1), :] = jnp.sum(ed * tau_f, axis=0, keepdims=True)
        return carry

    lax.fori_loop(0, modes, build, 0)
    d_all[me] = d_sum[:modes, :].astype(BF16)
    span(0, me, lambda j: d_copy(me, j).start())

    @pl.when(me == 0)
    def _():
        rim[...] = jnp.zeros_like(rim)

    @pl.when(me > 0)
    def _():
        rim_copy(me).wait_recv()

    xs = xs_ref[...] + sign * spectrum(rim[...])
    xs_ref[...] = xs
    mr = signal(times(fs_ref[...], xs, False)).astype(BF16)
    u = product(ig_ref[...], mr)
    u_ref[...] = u.astype(F32)

    def condense(m, carry):
        eu = decay_rev[m] * u_ref[...]
        u_sum[pl.ds(m, 1), :] = jnp.sum(eu, axis=0, keepdims=True)
        u_sum[pl.ds(modes + m, 1), :] = jnp.sum(eu * left_f, axis=0, keepdims=True)
        return carry

    lax.fori_loop(0, modes, condense, 0)
    u_all[me] = u_sum[...].astype(BF16)
    span(me + 1, n, lambda j: u_copy(me, j).start())

    h_hi, h_lo = split(h_ref[...])
    hs = spectrum(h_hi) + dot(fwd_hi, h_lo)
    us = spectrum(u)
    ds = spectrum(dz)
    back_ref[...] = signal(times(hs, ds, True))
    conv_ref[...] = signal(times(hs, us, False))
    g_ref[...] = signal(times(us, ds, True))

    step_decay = jnp.exp(-rates[...])
    jump = jnp.exp(-rates[...] * rows)

    span(me + 1, n, lambda j: d_copy(j, j).wait_recv())
    later = lax.fori_loop(
        0, n - 1 - me, lambda i, b: b * jump + d_all[n - 1 - i].astype(F32), jnp.zeros((modes, chans), F32)
    )
    m_sum[:modes, :] = resid[...] * step_decay * later

    def spread_back(m, carry):
        back_ref[...] += m_sum[pl.ds(m, 1), :] * decay_rev[m]
        return carry

    lax.fori_loop(0, modes, spread_back, 0)
    back = back_ref[...].astype(BF16)
    grad = product(back, ig_ref[...])
    dv[...] = grad

    @pl.when(me > 0)
    def _():
        dv_copy(me - 1).start()

    dvs = spectrum(grad)
    c_hi, c_lo = split(signal(times(xs_ref[...], dvs, True)))
    nt = (((1,), (1,)), ((), ()))
    fg_all[me] = lax.dot_general(member, c_hi, nt, preferred_element_type=F32) + lax.dot_general(
        member, c_lo, nt, preferred_element_type=F32
    )
    others(lambda j: fg_copy(me, j).start())
    igg_ref[...] = product(back, mr)

    span(0, me, lambda j: u_copy(j, j).wait_recv())

    def prior(j, carry):
        s, s1 = carry
        return (
            s * jump + u_all[j, :modes, :].astype(F32),
            (s1 + rows * s) * jump + u_all[j, modes:, :].astype(F32),
        )

    zero = jnp.zeros((modes, chans), F32)
    s, s1 = lax.fori_loop(0, me, prior, (zero, zero))
    s, s1 = s * step_decay, s1 * step_decay

    def lags(m, carry):
        eg = decay[m] * g_ref[...]
        m_sum[pl.ds(m, 1), :] = jnp.sum(eg, axis=0, keepdims=True)
        m_sum[pl.ds(modes + m, 1), :] = jnp.sum(eg * tau_f, axis=0, keepdims=True)
        return carry

    lax.fori_loop(0, modes, lags, 0)
    d0, d1 = d_sum[:modes, :], d_sum[modes:, :]
    m_sum[:modes, :] += s * d0
    m_sum[modes:, :] += s * (d0 + d1) + s1 * d0
    for j in range(n):
        for g in range(2 * parts):
            mp_send[j, :, g * own : (g + 1) * own] = m_sum[8 * g : 8 * g + 8, j * own : (j + 1) * own]
    mp_all[me] = mp_send[me]
    others(lambda j: mp_copy(me, j).start())

    u_sum[:modes, :] = resid[...] * s

    def spread_conv(m, carry):
        conv_ref[...] += u_sum[pl.ds(m, 1), :] * decay[m]
        return carry

    lax.fori_loop(0, modes, spread_conv, 0)
    ogg_ref[...] = product(oc_ref[...], conv_ref[...].astype(BF16))

    @pl.when(me == n - 1)
    def _():
        dv_rim[...] = jnp.zeros_like(dv_rim)

    @pl.when(me < n - 1)
    def _():
        dv_copy(me).wait_recv()

    ws = dvs + sign * spectrum(dv_rim[...])
    xg_ref[...] = signal(times(fs_ref[...], ws, True)).astype(BF16)

    scale = 1.0 / math.sqrt(rows * n)
    others(lambda j: fg_copy(j, j).wait_recv())
    fg_ref[...] = jnp.sum(fg_all[...], axis=0) * scale
    others(lambda j: mp_copy(j, j).wait_recv())
    total = jnp.sum(mp_all[...], axis=0)
    for g in range(parts):
        rate = rate_ref[8 * g : 8 * g + 8, :]
        gain = jnp.sqrt(2.0 * rate / modes)
        first = total[:, g * own : (g + 1) * own]
        second = total[:, (parts + g) * own : (parts + g + 1) * own]
        rg_ref[8 * g : 8 * g + 8, :] = gain * first * scale
        tg_ref[8 * g : 8 * g + 8, :] = res_ref[8 * g : 8 * g + 8, :] * gain * (0.5 * first - rate * second) * scale

    others(lambda j: rr_copy(me, j).wait_send())
    others(lambda j: fg_copy(me, j).wait_send())
    others(lambda j: mp_copy(me, j).wait_send())
    span(0, me, lambda j: d_copy(me, j).wait_send())
    span(me + 1, n, lambda j: u_copy(me, j).wait_send())

    @pl.when(me < n - 1)
    def _():
        rim_copy(me + 1).wait_send()

    @pl.when(me > 0)
    def _():
        dv_copy(me - 1).wait_send()


def local(x, og, ig, oc, filt, res, rate):
    n = lax.axis_size(AXIS)
    rows, chans = x.shape
    modes, own = rate.shape
    groups = filt.shape[1]
    assert rows == filt.shape[0] and 2 * (modes // 8) * own <= 128 and modes % 8 == 0
    fwd, inv = dft_tables(rows)
    vmem = pl.BlockSpec(memory_space=pltpu.VMEM)
    wide = (rows, chans)
    dma = pltpu.SemaphoreType.DMA
    out = pl.pallas_call(
        functools.partial(kernel, n),
        name="mixer",
        out_shape=(
            jax.ShapeDtypeStruct(wide, BF16),
            jax.ShapeDtypeStruct(wide, BF16),
            jax.ShapeDtypeStruct(wide, BF16),
            jax.ShapeDtypeStruct((groups, rows), F32),
            jax.ShapeDtypeStruct((modes, own), F32),
            jax.ShapeDtypeStruct((modes, own), F32),
        ),
        in_specs=[vmem] * 9,
        out_specs=(vmem,) * 6,
        scratch_shapes=[
            pltpu.VMEM(wide, BF16),
            pltpu.VMEM((n, 8, 128), F32),
            pltpu.VMEM((n, modes, chans), BF16),
            pltpu.VMEM((n, 2 * modes, chans), BF16),
            pltpu.VMEM(wide, BF16),
            pltpu.VMEM(wide, BF16),
            pltpu.VMEM((n, 8, 128), F32),
            pltpu.VMEM((n, 8, 128), F32),
            pltpu.VMEM((n, groups, rows), F32),
            pltpu.VMEM((modes, chans), F32),
            pltpu.VMEM((modes, chans), F32),
            pltpu.VMEM((modes,) + wide, F32),
            pltpu.VMEM((modes,) + wide, F32),
            pltpu.VMEM(wide, F32),
            pltpu.VMEM((2 * modes, chans), F32),
            pltpu.VMEM((2 * modes, chans), F32),
            pltpu.VMEM((2 * modes, chans), F32),
            pltpu.VMEM(wide, F32),
            pltpu.VMEM(wide, F32),
            pltpu.VMEM(wide, F32),
            pltpu.VMEM(wide, F32),
            pltpu.VMEM(wide, F32),
            pltpu.VMEM((2 * rows, chans), F32),
            pltpu.VMEM((2 * rows, chans), F32),
            dma((2,)), dma((n,)), dma((n,)), dma((n,)), dma((n,)), dma((n,)), dma((n,)), dma((2,)),
            dma((n,)), dma((n,)), dma((n,)), dma((n,)),
        ],
        compiler_params=pltpu.CompilerParams(
            collective_id=0, has_side_effects=True, vmem_limit_bytes=32 * 1024 * 1024
        ),
    )(x, og, ig, oc, filt, res, rate, jnp.asarray(fwd), jnp.asarray(inv))
    xg, ogg, igg, fg, rg, tg = out
    return xg, ogg, igg, fg.T, rg, tg


def solution(mesh):
    tokens = P("ctx", "ch")
    shared = P(None, "ch")
    owned = P(None, ("ch", "ctx"))
    return jax.shard_map(
        local,
        mesh=mesh,
        in_specs=(tokens, tokens, tokens, tokens, shared, owned, owned),
        out_specs=(tokens, tokens, tokens, shared, owned, owned),
        check_vma=False,
    )
```

time: 147 us -> 32.5 us (0.22)
  matrix products: 49 us -> 0 us
  starting transfers between devices: 28 us -> 0 us
  other arithmetic: 24 us -> 0 us
  blocking collectives: 23.6 us -> 0 us
  Pallas kernels: 0 us -> 21.8 us
  local copies, waits for them, and re-layouts: 17.7 us -> 9.67 us
    dot_general x41 -> x0, matrix products: 49 us -> none  [the longest x2 15.6 us: toeplitz(): jnp.einsum('bkj,jg->gbk', selector, filt, preferred_element_type=jnp.floa...]
    psum x1 -> x0, blocking collectives: 23.6 us -> none  [local(): filter_grad = lax.psum(local_sums, 'ctx') * (1.0 / math.sqrt(tokens_all))]
    all_to_all x4 -> x0, starting transfers between devices: 22.6 us -> none  [the longest x1 7.28 us: local(): lax.all_to_all(gated_cot, 'ctx', split_axis=1, concat_axis=0, tiled=True)]
    pallas_call x0 -> x1, Pallas kernels: none -> 21.8 us  [local(): pl.pallas_call(functools.partial(kernel, n), name='mixer', out_shape=(jax...]
    neg x32 -> x0, other arithmetic: 11.3 us -> none  [the longest x16 11.2 us: add_mode(): -rate[:, None] * tau[None, :]]
    reshape x7 -> x0, local copies, waits for them, and re-layouts: 7.02 us -> none  [the longest x1 3.74 us: local(): diagonals = jnp.sum(flat.reshape(local_groups, taps, 2 * taps + 1), axis=1)]
    ppermute x2 -> x0, starting transfers between devices: 5.46 us -> none  [from_behind(): return lax.ppermute(value, axis, pairs)]
    unnamed x28 -> x23, local copies, waits for them, and re-layouts: 5.64 us -> 9.67 us
  transfers between devices with their start and end apart: 6 -> 0, of which waited for: 2 -> 0; matrix products, arithmetic and copies ran while one was open for 42% -> 0% of each run, Pallas kernels for 0% -> 0%
where the time goes in v1:
time: 32.5 us; the launch traced here: 32.2 us
  Pallas kernels  21.8 us (67%)
  local copies, waits for them, and re-layouts  9.67 us (30%)
  between operations  0.68 us (2%)
    pallas_call x1, Pallas kernels, local(): pl.pallas_call(functools.partial(kernel, n), name='mixer', out_shape=(jax...  21.8 us
    unnamed x23, local copies, waits for them, and re-layouts  9.67 us

profile of v1, /device:TPU:0, one launch (start us, length us, event | category | flops | bytes accessed | tf_op | source)
XLA Modules:
  0.0 32.2 jit_solution(18217022856468143517)
XLA Ops:
  0.6 0.0 copy-start.7
  0.6 0.0 copy-start.6
  0.7 0.8 %copy.15.filt_ref = bf16[128,16]{1,0:T(8,128)(2,1)S(1)} copy(bf16[128,16]{0,1:T(8,128)(2,1)} %param.13) | data formatting | bytes 8192 | tf_op args[4]
  1.5 0.0 copy-done.7
  1.5 0.0 copy-done.6
  1.5 0.0 copy-start
  1.5 0.9 %copy-done = bf16[256,256]{1,0:T(8,128)(2,1)S(1)} copy-done((bf16[256,256]{1,0:T(8,128)(2,1)S(1)}, bf16[256,256]{1,0:T(8,128)(2,1)}, u32[]{:S(2)}) %copy-start) | copy-done | bytes 131096
  2.4 0.0 copy-start.1
  2.4 0.9 %copy-done.1 = bf16[256,256]{1,0:T(8,128)(2,1)S(1)} copy-done((bf16[256,256]{1,0:T(8,128)(2,1)S(1)}, bf16[256,256]{1,0:T(8,128)(2,1)}, u32[]{:S(2)}) %copy-start.1) | copy-done | bytes 131096
  3.3 0.0 copy-start.2
  3.3 0.8 %copy-done.2 = bf16[128,256]{1,0:T(8,128)(2,1)S(1)} copy-done((bf16[128,256]{1,0:T(8,128)(2,1)S(1)}, bf16[128,256]{1,0:T(8,128)(2,1)}, u32[]{:S(2)}) %copy-start.2) | copy-done | bytes 65560
  4.1 0.0 copy-start.3
  4.1 0.8 %copy-done.3 = bf16[128,256]{1,0:T(8,128)(2,1)S(1)} copy-done((bf16[128,256]{1,0:T(8,128)(2,1)S(1)}, bf16[128,256]{1,0:T(8,128)(2,1)}, u32[]{:S(2)}) %copy-start.3) | copy-done | bytes 65560
  5.0 0.0 copy-start.4
  5.0 0.8 %copy-done.4 = bf16[128,256]{1,0:T(8,128)(2,1)S(1)} copy-done((bf16[128,256]{1,0:T(8,128)(2,1)S(1)}, bf16[128,256]{1,0:T(8,128)(2,1)}, u32[]{:S(2)}) %copy-start.4) | copy-done | bytes 65560
  5.8 0.0 copy-start.5
  5.8 0.8 %copy-done.5 = bf16[128,256]{1,0:T(8,128)(2,1)S(1)} copy-done((bf16[128,256]{1,0:T(8,128)(2,1)S(1)}, bf16[128,256]{1,0:T(8,128)(2,1)}, u32[]{:S(2)}) %copy-start.5) | copy-done | bytes 65560
  6.7 21.8 %mixer.1 = (bf16[128,256]{1,0:T(8,128)(2,1)S(1)}, bf16[128,256]{1,0:T(8,128)(2,1)S(1)}, bf16[128,256]{1,0:T(8,128)(2,1)S(1)}, f32[16,128]{1,0:T(8,128)S(1)}, f32[16,32]{1,0:T(8,128)S(1)}, /*index=5*/f32[16,32]{1,0:T(8,128)S(1)}) custom-call(bf16[128,256]{1,0:T(8,128)(2,1)S(1)} %copy-done.2, bf16[128,256]{1,0:T(8,128)(2,1)S(1)} %copy-done.3, ...), custom_call_target="tpu_custom_call" | custom-call | tf_op jit(solution)/shard_map/mixer/pallas_call | solution.py:333
  28.5 0.6 %copy.22 = bf16[128,256]{1,0:T(8,128)(2,1)} copy(bf16[128,256]{1,0:T(8,128)(2,1)S(1)} %get-tuple-element.24) | data formatting | bytes 131072
  29.1 0.6 %copy.23 = bf16[128,256]{1,0:T(8,128)(2,1)} copy(bf16[128,256]{1,0:T(8,128)(2,1)S(1)} %get-tuple-element.25) | data formatting | bytes 131072
  29.7 0.6 %copy.24 = bf16[128,256]{1,0:T(8,128)(2,1)} copy(bf16[128,256]{1,0:T(8,128)(2,1)S(1)} %get-tuple-element.26) | data formatting | bytes 131072
  30.4 0.6 %copy.25 = f32[128,16]{0,1:T(8,128)} copy(f32[128,16]{0,1:T(8,128)S(1)} %bitcast.1) | data formatting | bytes 16384
  31.0 0.6 %copy.26 = f32[16,32]{1,0:T(8,128)} copy(f32[16,32]{1,0:T(8,128)S(1)} %get-tuple-element.28) | data formatting | bytes 4096
  31.6 0.6 %copy.27 = f32[16,32]{1,0:T(8,128)} copy(f32[16,32]{1,0:T(8,128)S(1)} %get-tuple-element.29) | data formatting | bytes 4096
Async XLA Ops:
  0.6 0.8 %copy-start.7 = (f32[16,32]{1,0:T(8,128)S(1)}, f32[16,32]{1,0:T(8,128)}, u32[]{:S(2)}) copy-start(f32[16,32]{1,0:T(8,128)} %rate_ref.1) | copy-start | bytes 6148
  0.6 0.8 %copy-start.6 = (f32[16,32]{1,0:T(8,128)S(1)}, f32[16,32]{1,0:T(8,128)}, u32[]{:S(2)}) copy-start(f32[16,32]{1,0:T(8,128)} %res_ref.1) | copy-start | bytes 6148
  1.5 0.9 %copy-start = (bf16[256,256]{1,0:T(8,128)(2,1)S(1)}, bf16[256,256]{1,0:T(8,128)(2,1)}, u32[]{:S(2)}) copy-start(bf16[256,256]{1,0:T(8,128)(2,1)} %constant.5.clone.inv_ref) | copy-start | bytes 393220
  2.4 0.9 %copy-start.1 = (bf16[256,256]{1,0:T(8,128)(2,1)S(1)}, bf16[256,256]{1,0:T(8,128)(2,1)}, u32[]{:S(2)}) copy-start(bf16[256,256]{1,0:T(8,128)(2,1)} %constant.4.clone.fwd_ref) | copy-start | bytes 393220
  3.3 0.8 %copy-start.2 = (bf16[128,256]{1,0:T(8,128)(2,1)S(1)}, bf16[128,256]{1,0:T(8,128)(2,1)}, u32[]{:S(2)}) copy-start(bf16[128,256]{1,0:T(8,128)(2,1)} %x_ref.1) | copy-start | bytes 196612
  4.1 0.8 %copy-start.3 = (bf16[128,256]{1,0:T(8,128)(2,1)S(1)}, bf16[128,256]{1,0:T(8,128)(2,1)}, u32[]{:S(2)}) copy-start(bf16[128,256]{1,0:T(8,128)(2,1)} %og_ref.1) | copy-start | bytes 196612
  5.0 0.8 %copy-start.4 = (bf16[128,256]{1,0:T(8,128)(2,1)S(1)}, bf16[128,256]{1,0:T(8,128)(2,1)}, u32[]{:S(2)}) copy-start(bf16[128,256]{1,0:T(8,128)(2,1)} %ig_ref.1) | copy-start | bytes 196612
  5.8 0.8 %copy-start.5 = (bf16[128,256]{1,0:T(8,128)(2,1)S(1)}, bf16[128,256]{1,0:T(8,128)(2,1)}, u32[]{:S(2)}) copy-start(bf16[128,256]{1,0:T(8,128)(2,1)} %oc_ref.1) | copy-start | bytes 196612

commit v2 on v1

--- a/solution.py
+++ b/solution.py
@@ -12,6 +12,7 @@
 MESH = pl.DeviceIdType.MESH
 F32, BF16 = jnp.float32, jnp.bfloat16
 AXIS = "ctx"
+GRANT = 60 * 1024 * 1024
 
 
 def dft_tables(half):
@@ -48,17 +49,29 @@
 
 
 def kernel(
-    n, x_ref, og_ref, ig_ref, oc_ref, filt_ref, res_ref, rate_ref, fwd_ref, inv_ref,
-    xg_ref, ogg_ref, igg_ref, fg_ref, rg_ref, tg_ref,
-    rim, rr_all, d_all, u_all, dv, dv_rim, mp_send, mp_all, fg_all,
+    n, x_hbm, og_hbm, ig_hbm, oc_hbm, filt_hbm, res_hbm, rate_hbm, fwd_hbm, inv_hbm,
+    xg_hbm, ogg_hbm, igg_hbm, fg_hbm, rg_hbm, tg_hbm,
+    xg_ref, ogg_ref, igg_ref, fg_ref, rg_ref, tg_ref, out_sem, rim, rr_all, d_all, u_all, dv, dv_rim, mp_send, mp_all, fg_all,
     rates, resid, decay, decay_rev, h_ref, d_sum, u_sum, m_sum, dz_ref, u_ref, g_ref,
     back_ref, conv_ref, xs_ref, fs_ref,
+    x_ref, og_ref, ig_ref, oc_ref, filt_ref, res_ref, rate_ref, fwd_ref, inv_ref, in_sem,
     rim_sem, rr_send, rr_recv, d_send, d_recv, u_send, u_recv, dv_sem, mp_ssem, mp_rsem, fg_send, fg_recv,
 ):
+    order = (
+        (rate_hbm, rate_ref), (res_hbm, res_ref), (x_hbm, x_ref), (filt_hbm, filt_ref), (fwd_hbm, fwd_ref),
+        (og_hbm, og_ref), (oc_hbm, oc_ref), (ig_hbm, ig_ref), (inv_hbm, inv_ref),
+    )
+    loads = [pltpu.make_async_copy(src, dst, in_sem.at[i]) for i, (src, dst) in enumerate(order)]
+    for load in loads:
+        load.start()
+    finals = (
+        (xg_ref, xg_hbm), (ogg_ref, ogg_hbm), (igg_ref, igg_hbm), (fg_ref, fg_hbm), (rg_ref, rg_hbm), (tg_ref, tg_hbm)
+    )
+    puts = [pltpu.make_async_copy(src, dst, out_sem.at[i]) for i, (src, dst) in enumerate(finals)]
     me = lax.axis_index(AXIS)
     rows, chans = x_ref.shape
     modes, own = rate_ref.shape
-    groups = filt_ref.shape[1]
+    groups = filt_ref.shape[0]
     parts = modes // 8
 
     barrier = pltpu.get_barrier_semaphore()
@@ -68,6 +81,8 @@
         return carry
 
     lax.fori_loop(1, n, greet, 0)
+    loads[0].wait()
+    loads[1].wait()
     for g in range(parts):
         rr_all[me, :, g * own : (g + 1) * own] = rate_ref[8 * g : 8 * g + 8, :]
         rr_all[me, :, (parts + g) * own : (parts + g + 1) * own] = res_ref[8 * g : 8 * g + 8, :]
@@ -114,11 +129,14 @@
         lax.fori_loop(lo, hi, step, 0)
 
     others(lambda j: rr_copy(me, j).start())
+    loads[2].wait()
 
     @pl.when(me < n - 1)
     def _():
         rim_copy(me + 1).start()
 
+    for load in loads[3:]:
+        load.wait()
     fwd = fwd_ref[...]
     fwd_hi = fwd[:, :rows]
     inv_hi = inv_ref[:rows, :]
@@ -148,7 +166,9 @@
         lax.broadcasted_iota(jnp.int32, (groups, chans), 1) // (chans // groups)
         == lax.broadcasted_iota(jnp.int32, (groups, chans), 0)
     ).astype(BF16)
-    taps = dot(filt_ref[...], member).astype(BF16)
+    taps = lax.dot_general(
+        filt_ref[...], member, (((0,), (0,)), ((), ())), preferred_element_type=F32
+    ).astype(BF16)
     fs_ref[...] = spectrum(taps)
     dz = product(og_ref[...], oc_ref[...])
     dz_ref[...] = dz.astype(F32)
@@ -242,6 +262,7 @@
     )
     others(lambda j: fg_copy(me, j).start())
     igg_ref[...] = product(back, mr)
+    puts[2].start()
 
     span(0, me, lambda j: u_copy(j, j).wait_recv())
 
@@ -280,6 +301,7 @@
 
     lax.fori_loop(0, modes, spread_conv, 0)
     ogg_ref[...] = product(oc_ref[...], conv_ref[...].astype(BF16))
+    puts[1].start()
 
     @pl.when(me == n - 1)
     def _():
@@ -291,10 +313,12 @@
 
     ws = dvs + sign * spectrum(dv_rim[...])
     xg_ref[...] = signal(times(fs_ref[...], ws, True)).astype(BF16)
+    puts[0].start()
 
     scale = 1.0 / math.sqrt(rows * n)
     others(lambda j: fg_copy(j, j).wait_recv())
     fg_ref[...] = jnp.sum(fg_all[...], axis=0) * scale
+    puts[3].start()
     others(lambda j: mp_copy(j, j).wait_recv())
     total = jnp.sum(mp_all[...], axis=0)
     for g in range(parts):
@@ -304,6 +328,8 @@
         second = total[:, (parts + g) * own : (parts + g + 1) * own]
         rg_ref[8 * g : 8 * g + 8, :] = gain * first * scale
         tg_ref[8 * g : 8 * g + 8, :] = res_ref[8 * g : 8 * g + 8, :] * gain * (0.5 * first - rate * second) * scale
+    puts[4].start()
+    puts[5].start()
 
     others(lambda j: rr_copy(me, j).wait_send())
     others(lambda j: fg_copy(me, j).wait_send())
@@ -318,6 +344,23 @@
     @pl.when(me > 0)
     def _():
         dv_copy(me - 1).wait_send()
+
+    for put in puts:
+        put.wait()
+
+
+def store(*refs):
+    count = (len(refs) - 2) // 3
+    sources, targets, holds = refs[:count], refs[count : 2 * count], refs[2 * count : 3 * count]
+    takes = [pltpu.make_async_copy(sources[i], holds[i], refs[-2].at[i]) for i in range(count)]
+    gives = [pltpu.make_async_copy(holds[i], targets[i], refs[-1].at[i]) for i in range(count)]
+    for take in takes:
+        take.start()
+    for take, give in zip(takes, gives):
+        take.wait()
+        give.start()
+    for give in gives:
+        give.wait()
 
 
 def local(x, og, ig, oc, filt, res, rate):
@@ -327,7 +370,7 @@
     groups = filt.shape[1]
     assert rows == filt.shape[0] and 2 * (modes // 8) * own <= 128 and modes % 8 == 0
     fwd, inv = dft_tables(rows)
-    vmem = pl.BlockSpec(memory_space=pltpu.VMEM)
+    hbm = pl.BlockSpec(memory_space=pltpu.HBM)
     wide = (rows, chans)
     dma = pltpu.SemaphoreType.DMA
     out = pl.pallas_call(
@@ -341,9 +384,11 @@
             jax.ShapeDtypeStruct((modes, own), F32),
             jax.ShapeDtypeStruct((modes, own), F32),
         ),
-        in_specs=[vmem] * 9,
-        out_specs=(vmem,) * 6,
+        in_specs=[hbm] * 9,
+        out_specs=(hbm,) * 6,
         scratch_shapes=[
+            pltpu.VMEM(wide, BF16), pltpu.VMEM(wide, BF16), pltpu.VMEM(wide, BF16), pltpu.VMEM((groups, rows), F32),
+            pltpu.VMEM((modes, own), F32), pltpu.VMEM((modes, own), F32), dma((6,)),
             pltpu.VMEM(wide, BF16),
             pltpu.VMEM((n, 8, 128), F32),
             pltpu.VMEM((n, modes, chans), BF16),
@@ -368,14 +413,25 @@
             pltpu.VMEM(wide, F32),
             pltpu.VMEM((2 * rows, chans), F32),
             pltpu.VMEM((2 * rows, chans), F32),
+            pltpu.VMEM(wide, BF16), pltpu.VMEM(wide, BF16), pltpu.VMEM(wide, BF16), pltpu.VMEM(wide, BF16),
+            pltpu.VMEM((groups, rows), BF16), pltpu.VMEM((modes, own), F32), pltpu.VMEM((modes, own), F32),
+            pltpu.VMEM(fwd.shape, BF16), pltpu.VMEM(inv.shape, BF16), dma((9,)),
             dma((2,)), dma((n,)), dma((n,)), dma((n,)), dma((n,)), dma((n,)), dma((n,)), dma((2,)),
             dma((n,)), dma((n,)), dma((n,)), dma((n,)),
         ],
         compiler_params=pltpu.CompilerParams(
-            collective_id=0, has_side_effects=True, vmem_limit_bytes=32 * 1024 * 1024
+            collective_id=0, has_side_effects=True, vmem_limit_bytes=GRANT
         ),
-    )(x, og, ig, oc, filt, res, rate, jnp.asarray(fwd), jnp.asarray(inv))
-    xg, ogg, igg, fg, rg, tg = out
+    )(x, og, ig, oc, filt.T, res, rate, jnp.asarray(fwd), jnp.asarray(inv))
+    xg, ogg, igg, fg, rg, tg = pl.pallas_call(
+        store,
+        name="store",
+        out_shape=tuple(jax.ShapeDtypeStruct(o.shape, o.dtype) for o in out),
+        in_specs=[hbm] * 6,
+        out_specs=(hbm,) * 6,
+        scratch_shapes=[pltpu.VMEM(o.shape, o.dtype) for o in out] + [dma((6,)), dma((6,))],
+        compiler_params=pltpu.CompilerParams(vmem_limit_bytes=GRANT),
+    )(*out)
     return xg, ogg, igg, fg.T, rg, tg
 
 

time: 32.5 us -> 25.1 us (0.77)
  local copies, waits for them, and re-layouts: 9.67 us -> 0 us
  Pallas kernels: 21.8 us -> 24.2 us
    unnamed x23 -> x0, local copies, waits for them, and re-layouts: 9.67 us -> none
    pallas_call x0 -> x1, Pallas kernels: none -> 1.64 us  [local(): pl.pallas_call(store, name='store', out_shape=tuple((jax.ShapeDtypeStruct...]
    pallas_call x1, Pallas kernels: 21.8 us -> 22.6 us  [local(): pl.pallas_call(functools.partial(kernel, n), name='mixer', out_shape=(jax...]
where the time goes in v2:
time: 25.1 us; the launch traced here: 24.9 us
  Pallas kernels  24.2 us (96%)
  between operations  0.64 us (3%)
    pallas_call x1, Pallas kernels, local(): pl.pallas_call(functools.partial(kernel, n), name='mixer', out_shape=(jax...  22.6 us
    pallas_call x1, Pallas kernels, local(): pl.pallas_call(store, name='store', out_shape=tuple((jax.ShapeDtypeStruct...  1.64 us

profile of v2, /device:TPU:0, one launch (start us, length us, event | category | flops | bytes accessed | tf_op | source)
XLA Modules:
  0.0 24.9 jit_solution(5456182954370373592)
XLA Ops:
  0.6 22.6 %mixer.1 = (bf16[128,256]{1,0:T(8,128)(2,1)}, bf16[128,256]{1,0:T(8,128)(2,1)}, bf16[128,256]{1,0:T(8,128)(2,1)}, f32[16,128]{1,0:T(8,128)}, f32[16,32]{1,0:T(8,128)}, /*index=5*/f32[16,32]{1,0:T(8,128)}) custom-call(bf16[128,256]{1,0:T(8,128)(2,1)} %x_hbm.1, bf16[128,256]{1,0:T(8,128)(2,1)} %og_hbm.1, bf16[128,256]{1,0:T(8,128)(2,1)} %ig_hbm.1, ...), custom_call_target="tpu_custom_call" | custom-call | tf_op jit(solution)/shard_map/mixer/pallas_call | solution.py:376
  23.2 1.6 %store.1 = (bf16[128,256]{1,0:T(8,128)(2,1)}, bf16[128,256]{1,0:T(8,128)(2,1)}, bf16[128,256]{1,0:T(8,128)(2,1)}, f32[16,128]{1,0:T(8,128)}, f32[16,32]{1,0:T(8,128)}, /*index=5*/f32[16,32]{1,0:T(8,128)}) custom-call(bf16[128,256]{1,0:T(8,128)(2,1)} %get-tuple-element.18.refs_0_, bf16[128,256]{1,0:T(8,128)(2,1)} %get-tuple-element.19.refs_1_, ...), custom_call_target="tpu_custom_call" | custom-call | tf_op jit(solution)/shard_map/store/pallas_call | solution.py:426

commit v3 on v2

--- a/solution.py
+++ b/solution.py
@@ -53,7 +53,7 @@
     xg_hbm, ogg_hbm, igg_hbm, fg_hbm, rg_hbm, tg_hbm,
     xg_ref, ogg_ref, igg_ref, fg_ref, rg_ref, tg_ref, out_sem, rim, rr_all, d_all, u_all, dv, dv_rim, mp_send, mp_all, fg_all,
     rates, resid, decay, decay_rev, h_ref, d_sum, u_sum, m_sum, dz_ref, u_ref, g_ref,
-    back_ref, conv_ref, xs_ref, fs_ref,
+    back_ref, conv_ref, xs_ref, fs_ref, mr_ref,
     x_ref, og_ref, ig_ref, oc_ref, filt_ref, res_ref, rate_ref, fwd_ref, inv_ref, in_sem,
     rim_sem, rr_send, rr_recv, d_send, d_recv, u_send, u_recv, dv_sem, mp_ssem, mp_rsem, fg_send, fg_recv,
 ):
@@ -143,8 +143,6 @@
     inv_lo = inv_ref[rows:, :]
     tau = lax.broadcasted_iota(jnp.int32, (rows, chans), 0)
     first_row = tau == 0
-    tau_f = tau.astype(F32)
-    left_f = (rows - 1) - tau_f
     sign = (1 - 2 * lax.rem(lax.broadcasted_iota(jnp.int32, (2 * rows, chans), 0), 2)).astype(F32)
 
     def spectrum(value):
@@ -183,20 +181,68 @@
 
     norm = jnp.sqrt(2.0 * rates[...] / modes)
     resid[...] = resid[...] * norm
-    h_ref[...] = jnp.zeros_like(h_ref)
-
-    def build(m, carry):
-        rate = rates[pl.ds(m, 1), :]
-        e = jnp.exp(-rate * tau_f)
-        decay[m] = e
-        decay_rev[m] = jnp.exp(-rate * left_f)
-        h_ref[...] += resid[pl.ds(m, 1), :] * e
-        ed = e * dz_ref[...]
-        d_sum[pl.ds(m, 1), :] = jnp.sum(ed, axis=0, keepdims=True)
-        d_sum[pl.ds(modes + m, 1), :] = jnp.sum(ed * tau_f, axis=0, keepdims=True)
+    tiles = rows // 8
+    low = lax.broadcasted_iota(jnp.int32, (8, chans), 0).astype(F32)
+    high = 7.0 - low
+    batch = 4
+
+    def put_moments(sums, m, first, second):
+        sums[pl.ds(m, 1), :] = jnp.sum(first, axis=0, keepdims=True)
+        sums[pl.ds(modes + m, 1), :] = jnp.sum(second, axis=0, keepdims=True)
+
+    def build(group, carry):
+        for i in range(batch):
+            m = group * batch + i
+            rate = jnp.broadcast_to(rates[pl.ds(m, 1), :], (8, chans))
+            hop = jnp.exp(-8.0 * rate)
+            e = jnp.exp(-rate * low)
+            e_rev = jnp.exp(-rate * high)
+            first = run = jnp.zeros((8, chans), F32)
+            for t in range(tiles):
+                decay[m, 8 * t : 8 * t + 8, :] = e
+                decay_rev[m, rows - 8 * t - 8 : rows - 8 * t, :] = e_rev
+                first += e * dz_ref[8 * t : 8 * t + 8, :]
+                if t < tiles - 1:
+                    run += first
+                    e, e_rev = e * hop, e_rev * hop
+            put_moments(d_sum, m, first, 8.0 * ((tiles - 1) * first - run) + low * first)
         return carry
 
-    lax.fori_loop(0, modes, build, 0)
+    lax.fori_loop(0, modes // batch, build, 0)
+
+    def moments(sums, table, value, back):
+        def step(group, carry):
+            first = [jnp.zeros((8, chans), F32)] * batch
+            run = list(first)
+            for t in range(tiles):
+                part = value[8 * t : 8 * t + 8, :]
+                for i in range(batch):
+                    first[i] += table[group * batch + i, 8 * t : 8 * t + 8, :] * part
+                    if t < tiles - 1:
+                        run[i] += first[i]
+            for i in range(batch):
+                if back:
+                    second = 8.0 * run[i] + high * first[i]
+                else:
+                    second = 8.0 * ((tiles - 1) * first[i] - run[i]) + low * first[i]
+                put_moments(sums, group * batch + i, first[i], second)
+            return carry
+
+        lax.fori_loop(0, modes // batch, step, 0)
+
+    def blend(coef, table, at):
+        parts = [coef[m : m + 1, :] * table[m, at, :] for m in range(modes)]
+        while len(parts) > 1:
+            parts = [left + right for left, right in zip(parts[::2], parts[1::2])]
+        return parts[0]
+
+    def blocks(act):
+        def step(i, carry):
+            act(pl.ds(pl.multiple_of(16 * i, 16), 16))
+            return carry
+
+        lax.fori_loop(0, rows // 16, step, 0)
+
     d_all[me] = d_sum[:modes, :].astype(BF16)
     span(0, me, lambda j: d_copy(me, j).start())
 
@@ -211,19 +257,18 @@
     xs = xs_ref[...] + sign * spectrum(rim[...])
     xs_ref[...] = xs
     mr = signal(times(fs_ref[...], xs, False)).astype(BF16)
+    mr_ref[...] = mr
     u = product(ig_ref[...], mr)
     u_ref[...] = u.astype(F32)
 
-    def condense(m, carry):
-        eu = decay_rev[m] * u_ref[...]
-        u_sum[pl.ds(m, 1), :] = jnp.sum(eu, axis=0, keepdims=True)
-        u_sum[pl.ds(modes + m, 1), :] = jnp.sum(eu * left_f, axis=0, keepdims=True)
-        return carry
-
-    lax.fori_loop(0, modes, condense, 0)
+    moments(u_sum, decay_rev, u_ref, True)
     u_all[me] = u_sum[...].astype(BF16)
     span(me + 1, n, lambda j: u_copy(me, j).start())
 
+    def fill(at):
+        h_ref[at, :] = blend(resid, decay, at)
+
+    blocks(fill)
     h_hi, h_lo = split(h_ref[...])
     hs = spectrum(h_hi) + dot(fwd_hi, h_lo)
     us = spectrum(u)
@@ -241,28 +286,25 @@
     )
     m_sum[:modes, :] = resid[...] * step_decay * later
 
-    def spread_back(m, carry):
-        back_ref[...] += m_sum[pl.ds(m, 1), :] * decay_rev[m]
-        return carry
-
-    lax.fori_loop(0, modes, spread_back, 0)
-    back = back_ref[...].astype(BF16)
-    grad = product(back, ig_ref[...])
-    dv[...] = grad
+    def gates(at):
+        back = (back_ref[at, :] + blend(m_sum, decay_rev, at)).astype(BF16)
+        dv[at, :] = product(back, ig_ref[at, :])
+        igg_ref[at, :] = product(back, mr_ref[at, :])
+
+    blocks(gates)
 
     @pl.when(me > 0)
     def _():
         dv_copy(me - 1).start()
 
-    dvs = spectrum(grad)
+    puts[2].start()
+    dvs = spectrum(dv[...])
     c_hi, c_lo = split(signal(times(xs_ref[...], dvs, True)))
     nt = (((1,), (1,)), ((), ()))
     fg_all[me] = lax.dot_general(member, c_hi, nt, preferred_element_type=F32) + lax.dot_general(
         member, c_lo, nt, preferred_element_type=F32
     )
     others(lambda j: fg_copy(me, j).start())
-    igg_ref[...] = product(back, mr)
-    puts[2].start()
 
     span(0, me, lambda j: u_copy(j, j).wait_recv())
 
@@ -277,13 +319,7 @@
     s, s1 = lax.fori_loop(0, me, prior, (zero, zero))
     s, s1 = s * step_decay, s1 * step_decay
 
-    def lags(m, carry):
-        eg = decay[m] * g_ref[...]
-        m_sum[pl.ds(m, 1), :] = jnp.sum(eg, axis=0, keepdims=True)
-        m_sum[pl.ds(modes + m, 1), :] = jnp.sum(eg * tau_f, axis=0, keepdims=True)
-        return carry
-
-    lax.fori_loop(0, modes, lags, 0)
+    moments(m_sum, decay, g_ref, False)
     d0, d1 = d_sum[:modes, :], d_sum[modes:, :]
     m_sum[:modes, :] += s * d0
     m_sum[modes:, :] += s * (d0 + d1) + s1 * d0
@@ -295,12 +331,11 @@
 
     u_sum[:modes, :] = resid[...] * s
 
-    def spread_conv(m, carry):
-        conv_ref[...] += u_sum[pl.ds(m, 1), :] * decay[m]
-        return carry
-
-    lax.fori_loop(0, modes, spread_conv, 0)
-    ogg_ref[...] = product(oc_ref[...], conv_ref[...].astype(BF16))
+    def emit(at):
+        conv = (conv_ref[at, :] + blend(u_sum, decay, at)).astype(BF16)
+        ogg_ref[at, :] = product(oc_ref[at, :], conv)
+
+    blocks(emit)
     puts[1].start()
 
     @pl.when(me == n - 1)
@@ -368,7 +403,7 @@
     rows, chans = x.shape
     modes, own = rate.shape
     groups = filt.shape[1]
-    assert rows == filt.shape[0] and 2 * (modes // 8) * own <= 128 and modes % 8 == 0
+    assert rows == filt.shape[0] and modes & (modes - 1) == 0 and 2 * (modes // 8) * own <= 128 and modes % 8 == 0
     fwd, inv = dft_tables(rows)
     hbm = pl.BlockSpec(memory_space=pltpu.HBM)
     wide = (rows, chans)
@@ -413,6 +448,7 @@
             pltpu.VMEM(wide, F32),
             pltpu.VMEM((2 * rows, chans), F32),
             pltpu.VMEM((2 * rows, chans), F32),
+            pltpu.VMEM(wide, BF16),
             pltpu.VMEM(wide, BF16), pltpu.VMEM(wide, BF16), pltpu.VMEM(wide, BF16), pltpu.VMEM(wide, BF16),
             pltpu.VMEM((groups, rows), BF16), pltpu.VMEM((modes, own), F32), pltpu.VMEM((modes, own), F32),
             pltpu.VMEM(fwd.shape, BF16), pltpu.VMEM(inv.shape, BF16), dma((9,)),

time: 25.1 us -> 23.9 us (0.952)
  Pallas kernels: 24.2 us -> 23.1 us
    pallas_call x1, Pallas kernels: 22.6 us -> 21.4 us  [local(): pl.pallas_call(functools.partial(kernel, n), name='mixer', out_shape=(jax...]
where the time goes in v3:
time: 23.9 us; the launch traced here: 23.7 us
  Pallas kernels  23.1 us (97%)
  between operations  0.64 us (3%)
    pallas_call x1, Pallas kernels, local(): pl.pallas_call(functools.partial(kernel, n), name='mixer', out_shape=(jax...  21.4 us
    pallas_call x1, Pallas kernels, local(): pl.pallas_call(store, name='store', out_shape=tuple((jax.ShapeDtypeStruct...  1.64 us

profile of v3, /device:TPU:0, one launch (start us, length us, event | category | flops | bytes accessed | tf_op | source)
XLA Modules:
  0.0 23.7 jit_solution(495042026618052891)
XLA Ops:
  0.6 21.4 %mixer.1 = (bf16[128,256]{1,0:T(8,128)(2,1)}, bf16[128,256]{1,0:T(8,128)(2,1)}, bf16[128,256]{1,0:T(8,128)(2,1)}, f32[16,128]{1,0:T(8,128)}, f32[16,32]{1,0:T(8,128)}, /*index=5*/f32[16,32]{1,0:T(8,128)}) custom-call(bf16[128,256]{1,0:T(8,128)(2,1)} %x_hbm.1, bf16[128,256]{1,0:T(8,128)(2,1)} %og_hbm.1, bf16[128,256]{1,0:T(8,128)(2,1)} %ig_hbm.1, ...), custom_call_target="tpu_custom_call" | custom-call | tf_op jit(solution)/shard_map/mixer/pallas_call | solution.py:411
  22.1 1.6 %store.1 = (bf16[128,256]{1,0:T(8,128)(2,1)}, bf16[128,256]{1,0:T(8,128)(2,1)}, bf16[128,256]{1,0:T(8,128)(2,1)}, f32[16,128]{1,0:T(8,128)}, f32[16,32]{1,0:T(8,128)}, /*index=5*/f32[16,32]{1,0:T(8,128)}) custom-call(bf16[128,256]{1,0:T(8,128)(2,1)} %get-tuple-element.18.refs_0_, bf16[128,256]{1,0:T(8,128)(2,1)} %get-tuple-element.19.refs_1_, ...), custom_call_target="tpu_custom_call" | custom-call | tf_op jit(solution)/shard_map/store/pallas_call | solution.py:462

commit v4 on v3

--- a/solution.py
+++ b/solution.py
@@ -52,7 +52,7 @@
     n, x_hbm, og_hbm, ig_hbm, oc_hbm, filt_hbm, res_hbm, rate_hbm, fwd_hbm, inv_hbm,
     xg_hbm, ogg_hbm, igg_hbm, fg_hbm, rg_hbm, tg_hbm,
     xg_ref, ogg_ref, igg_ref, fg_ref, rg_ref, tg_ref, out_sem, rim, rr_all, d_all, u_all, dv, dv_rim, mp_send, mp_all, fg_all,
-    rates, resid, decay, decay_rev, h_ref, d_sum, u_sum, m_sum, dz_ref, u_ref, g_ref,
+    rates, resid, decay, decay_rev, coef, h_ref, d_sum, u_sum, m_sum, dz_ref, u_ref, g_ref,
     back_ref, conv_ref, xs_ref, fs_ref, mr_ref,
     x_ref, og_ref, ig_ref, oc_ref, filt_ref, res_ref, rate_ref, fwd_ref, inv_ref, in_sem,
     rim_sem, rr_send, rr_recv, d_send, d_recv, u_send, u_recv, dv_sem, mp_ssem, mp_rsem, fg_send, fg_recv,
@@ -230,8 +230,8 @@
 
         lax.fori_loop(0, modes // batch, step, 0)
 
-    def blend(coef, table, at):
-        parts = [coef[m : m + 1, :] * table[m, at, :] for m in range(modes)]
+    def blend(weight, table, at):
+        parts = [weight[m : m + 1, :] * table[m, at, :] for m in range(modes)]
         while len(parts) > 1:
             parts = [left + right for left, right in zip(parts[::2], parts[1::2])]
         return parts[0]
@@ -262,7 +262,7 @@
     u_ref[...] = u.astype(F32)
 
     moments(u_sum, decay_rev, u_ref, True)
-    u_all[me] = u_sum[...].astype(BF16)
+    u_all[me] = u_sum[:modes, :].astype(BF16)
     span(me + 1, n, lambda j: u_copy(me, j).start())
 
     def fill(at):
@@ -274,8 +274,8 @@
     us = spectrum(u)
     ds = spectrum(dz)
     back_ref[...] = signal(times(hs, ds, True))
-    conv_ref[...] = signal(times(hs, us, False))
     g_ref[...] = signal(times(us, ds, True))
+    moments(m_sum, decay, g_ref, False)
 
     step_decay = jnp.exp(-rates[...])
     jump = jnp.exp(-rates[...] * rows)
@@ -284,10 +284,10 @@
     later = lax.fori_loop(
         0, n - 1 - me, lambda i, b: b * jump + d_all[n - 1 - i].astype(F32), jnp.zeros((modes, chans), F32)
     )
-    m_sum[:modes, :] = resid[...] * step_decay * later
+    coef[...] = resid[...] * step_decay * later
 
     def gates(at):
-        back = (back_ref[at, :] + blend(m_sum, decay_rev, at)).astype(BF16)
+        back = (back_ref[at, :] + blend(coef, decay_rev, at)).astype(BF16)
         dv[at, :] = product(back, ig_ref[at, :])
         igg_ref[at, :] = product(back, mr_ref[at, :])
 
@@ -301,38 +301,35 @@
     dvs = spectrum(dv[...])
     c_hi, c_lo = split(signal(times(xs_ref[...], dvs, True)))
     nt = (((1,), (1,)), ((), ()))
-    fg_all[me] = lax.dot_general(member, c_hi, nt, preferred_element_type=F32) + lax.dot_general(
-        member, c_lo, nt, preferred_element_type=F32
-    )
+    fg_all[me] = (
+        lax.dot_general(member, c_hi, nt, preferred_element_type=F32)
+        + lax.dot_general(member, c_lo, nt, preferred_element_type=F32)
+    ).astype(BF16)
     others(lambda j: fg_copy(me, j).start())
 
+    conv_ref[...] = signal(times(hs, us, False))
     span(0, me, lambda j: u_copy(j, j).wait_recv())
 
     def prior(j, carry):
-        s, s1 = carry
-        return (
-            s * jump + u_all[j, :modes, :].astype(F32),
-            (s1 + rows * s) * jump + u_all[j, modes:, :].astype(F32),
-        )
+        s, far = carry
+        return s * jump + u_all[j].astype(F32), (far + s) * jump
 
     zero = jnp.zeros((modes, chans), F32)
-    s, s1 = lax.fori_loop(0, me, prior, (zero, zero))
-    s, s1 = s * step_decay, s1 * step_decay
-
-    moments(m_sum, decay, g_ref, False)
+    s, far = lax.fori_loop(0, me, prior, (zero, zero))
+    s = s * step_decay
     d0, d1 = d_sum[:modes, :], d_sum[modes:, :]
     m_sum[:modes, :] += s * d0
-    m_sum[modes:, :] += s * (d0 + d1) + s1 * d0
+    m_sum[modes:, :] += s * (d0 + d1) + step_decay * (rows * far * d0 + u_sum[modes:, :] * later)
     for j in range(n):
         for g in range(2 * parts):
             mp_send[j, :, g * own : (g + 1) * own] = m_sum[8 * g : 8 * g + 8, j * own : (j + 1) * own]
     mp_all[me] = mp_send[me]
     others(lambda j: mp_copy(me, j).start())
 
-    u_sum[:modes, :] = resid[...] * s
+    coef[...] = resid[...] * s
 
     def emit(at):
-        conv = (conv_ref[at, :] + blend(u_sum, decay, at)).astype(BF16)
+        conv = (conv_ref[at, :] + blend(coef, decay, at)).astype(BF16)
         ogg_ref[at, :] = product(oc_ref[at, :], conv)
 
     blocks(emit)
@@ -352,7 +349,7 @@
 
     scale = 1.0 / math.sqrt(rows * n)
     others(lambda j: fg_copy(j, j).wait_recv())
-    fg_ref[...] = jnp.sum(fg_all[...], axis=0) * scale
+    fg_ref[...] = jnp.sum(fg_all[...].astype(F32), axis=0) * scale
     puts[3].start()
     others(lambda j: mp_copy(j, j).wait_recv())
     total = jnp.sum(mp_all[...], axis=0)
@@ -427,16 +424,17 @@
             pltpu.VMEM(wide, BF16),
             pltpu.VMEM((n, 8, 128), F32),
             pltpu.VMEM((n, modes, chans), BF16),
-            pltpu.VMEM((n, 2 * modes, chans), BF16),
+            pltpu.VMEM((n, modes, chans), BF16),
             pltpu.VMEM(wide, BF16),
             pltpu.VMEM(wide, BF16),
             pltpu.VMEM((n, 8, 128), F32),
             pltpu.VMEM((n, 8, 128), F32),
-            pltpu.VMEM((n, groups, rows), F32),
+            pltpu.VMEM((n, groups, rows), BF16),
             pltpu.VMEM((modes, chans), F32),
             pltpu.VMEM((modes, chans), F32),
             pltpu.VMEM((modes,) + wide, F32),
             pltpu.VMEM((modes,) + wide, F32),
+            pltpu.VMEM((modes, chans), F32),
             pltpu.VMEM(wide, F32),
             pltpu.VMEM((2 * modes, chans), F32),
             pltpu.VMEM((2 * modes, chans), F32),

time: 23.9 us -> 23.1 us (0.967)
  Pallas kernels: 23.1 us -> 22.2 us
    pallas_call x1, Pallas kernels: 21.4 us -> 20.6 us  [local(): pl.pallas_call(functools.partial(kernel, n), name='mixer', out_shape=(jax...]
where the time goes in v4:
time: 23.1 us; the launch traced here: 22.9 us
  Pallas kernels  22.2 us (96%)
  between operations  0.64 us (3%)
    pallas_call x1, Pallas kernels, local(): pl.pallas_call(functools.partial(kernel, n), name='mixer', out_shape=(jax...  20.6 us
    pallas_call x1, Pallas kernels, local(): pl.pallas_call(store, name='store', out_shape=tuple((jax.ShapeDtypeStruct...  1.64 us

profile of v4, /device:TPU:0, one launch (start us, length us, event | category | flops | bytes accessed | tf_op | source)
XLA Modules:
  0.0 22.9 jit_solution(17984732112355995341)
XLA Ops:
  0.6 20.6 %mixer.1 = (bf16[128,256]{1,0:T(8,128)(2,1)}, bf16[128,256]{1,0:T(8,128)(2,1)}, bf16[128,256]{1,0:T(8,128)(2,1)}, f32[16,128]{1,0:T(8,128)}, f32[16,32]{1,0:T(8,128)}, /*index=5*/f32[16,32]{1,0:T(8,128)}) custom-call(bf16[128,256]{1,0:T(8,128)(2,1)} %x_hbm.1, bf16[128,256]{1,0:T(8,128)(2,1)} %og_hbm.1, bf16[128,256]{1,0:T(8,128)(2,1)} %ig_hbm.1, ...), custom_call_target="tpu_custom_call" | custom-call | tf_op jit(solution)/shard_map/mixer/pallas_call | solution.py:408
  21.2 1.6 %store.1 = (bf16[128,256]{1,0:T(8,128)(2,1)}, bf16[128,256]{1,0:T(8,128)(2,1)}, bf16[128,256]{1,0:T(8,128)(2,1)}, f32[16,128]{1,0:T(8,128)}, f32[16,32]{1,0:T(8,128)}, /*index=5*/f32[16,32]{1,0:T(8,128)}) custom-call(bf16[128,256]{1,0:T(8,128)(2,1)} %get-tuple-element.18.refs_0_, bf16[128,256]{1,0:T(8,128)(2,1)} %get-tuple-element.19.refs_1_, ...), custom_call_target="tpu_custom_call" | custom-call | tf_op jit(solution)/shard_map/store/pallas_call | solution.py:460
